TPU v7x, 32 devices: a whole 2x2x4 slice. The times are simulated.
32 devices in a mesh: rep: 2 (over y), ctx: 4 (over z), ch: 2 (over x), sub: 2 (over core).
Axes of the slice: x: 2, y: 2, z: 4, core: 2. Of those that a mesh axis runs over, the one named last changes fastest.
Arguments:
- hyena_query: bfloat16 [3072, 8192], P(('rep', 'ctx'), ('ch', 'sub')), parts along dimension 0, may hold values from -6 to 6
- hyena_key: bfloat16 [3072, 8192], P(('rep', 'ctx'), ('ch', 'sub')), parts along dimension 0, may hold values from -6 to 6
- hyena_value: bfloat16 [3072, 8192], P(('rep', 'ctx'), ('ch', 'sub')), parts along dimension 0, may hold values from -6 to 6
- filters: bfloat16 [512, 128], P(('ch', 'sub')), may hold values from -0.5 to 0.5
- skip_gain: float32 [8192], P(('ch', 'sub')), may hold values from 0.5 to 1.5
- attn_query: bfloat16 [3072, 8192], P(('rep', 'ctx'), ('ch', 'sub')), parts along dimension 0, may hold values from -40 to 40
- attn_key: bfloat16 [3072, 8192], P(('rep', 'ctx'), ('ch', 'sub')), parts along dimension 0, may hold values from -5 to 5
- genome_starts: int32 [8], P('rep'), parts along dimension 0, may hold values from 0 to 1408, as said below
Outputs:
- hyena_mix: bfloat16 [3072, 8192], P(('rep', 'ctx'), ('ch', 'sub')), parts along dimension 0
- attended: bfloat16 [3072, 8192], P(('rep', 'ctx'), ('ch', 'sub')), parts along dimension 0
There are 2 independent parts, one for each index of `rep`. A program takes and returns all parts, laid end to end along the dimension named above; an argument that names none is the same for every part. Nothing has to cross between parts.
Inputs may be any that keep to these rules, and one draw needn't show every extreme that they name: genome_starts[0] is 0; the entries rise, each by 128 or more, and the last genome holds exactly 128 positions.
All inputs are finite; a program needn't handle non-finite values.
Results may differ from a plain program's by a relative error of at most 0.0059.
Values may be sent and summed in bfloat16 or wider, within the bound.
A program may use at most 128 MiB of HBM per device.

v0:
```python
from functools import partial
import math
import jax
import jax.numpy as jnp
from jax import lax
from jax.sharding import PartitionSpec as P

HEAD_DIM = 128


def passed_along(value, axis, by):
    devices = lax.axis_size(axis)
    pairs = [(i, i + by) for i in range(devices) if 0 <= i + by < devices]
    return lax.ppermute(value, axis, pairs)


def genome_index(positions, genome_starts):
    inside = genome_starts[None, :] <= positions[:, None]
    return jnp.sum(inside.astype(jnp.int32), axis=1) - 1


def genome_begin(positions, genome_starts):
    inside = genome_starts[None, :] <= positions[:, None]
    return jnp.max(jnp.where(inside, genome_starts[None, :], 0), axis=1)


def grouped_filter(product, parity, filters, left_pad):
    channels = product.shape[1]
    group_width = channels // filters.shape[0]
    kernel = jnp.repeat(filters, group_width, axis=0).T[::-1][:, None, :]
    nothing = jnp.zeros_like(product)
    even_rows = jnp.where((parity == 0)[:, None], product, nothing)
    odd_rows = jnp.where((parity == 1)[:, None], product, nothing)
    stacked = jnp.stack([even_rows, odd_rows])
    return lax.conv_general_dilated(
        stacked,
        kernel,
        (1,),
        [(left_pad, 0)],
        dimension_numbers=("NWC", "WIO", "NWC"),
        feature_group_count=channels,
        preferred_element_type=jnp.float32,
    )


def attend_update(carried, queries, query_pos, query_begin, key_heads, value_heads, key_pos):
    weighted, running_max, weight_sum = carried
    score_scale = 1.0 / math.sqrt(HEAD_DIM)
    scores = (
        jnp.einsum("qhd,khd->hqk", queries, key_heads, preferred_element_type=jnp.float32)
        * score_scale
    )
    visible = (key_pos[None, :] <= query_pos[:, None]) & (key_pos[None, :] >= query_begin[:, None])
    new_max = jnp.maximum(running_max, jnp.max(jnp.where(visible[None], scores, -1e30), axis=2))
    weights = jnp.exp(jnp.where(visible[None], scores - new_max[:, :, None], -1e30))
    mixed = jnp.einsum(
        "hqk,khd->hqd",
        weights.astype(jnp.bfloat16),
        value_heads,
        preferred_element_type=jnp.float32,
    )
    return (mixed, new_max, jnp.sum(weights, axis=2))


def keep_state(carried):
    return carried


def per_device(
    hyena_query, hyena_key, hyena_value, filters, skip_gain, attn_query, attn_key, genome_starts
):
    local_rows, channels = hyena_key.shape
    taps = filters.shape[1]
    shard_first = lax.axis_index("ctx") * local_rows
    product = lax.optimization_barrier(
        (hyena_key.astype(jnp.float32) * hyena_value.astype(jnp.float32)).astype(jnp.bfloat16)
    )
    earlier = passed_along(product[local_rows - (taps - 1) :], "ctx", 1)
    extended = jnp.concatenate([earlier, product], axis=0)
    extended_pos = shard_first - (taps - 1) + jnp.arange(local_rows + taps - 1, dtype=jnp.int32)
    both_parities = grouped_filter(
        extended, genome_index(extended_pos, genome_starts) % 2, filters, 0
    )
    own_pos = shard_first + jnp.arange(local_rows, dtype=jnp.int32)
    own_parity = genome_index(own_pos, genome_starts) % 2
    filtered = jnp.where((own_parity == 0)[:, None], both_parities[0], both_parities[1])
    hyena_mix = (
        hyena_query.astype(jnp.float32)
        * (filtered + skip_gain[None, :] * product.astype(jnp.float32))
    ).astype(jnp.bfloat16)
    head_count = channels // HEAD_DIM
    queries = attn_query.reshape(local_rows, head_count, HEAD_DIM)
    pairs = [(queries, own_pos)]
    groups = [
        (group_queries, group_pos, genome_begin(group_pos, genome_starts))
        for group_queries, group_pos in pairs
    ]
    initial = tuple(
        (
            (
                jnp.zeros((head_count, group_pos.shape[0], HEAD_DIM), jnp.float32),
                jnp.full((head_count, group_pos.shape[0]), -1e30, jnp.float32),
                jnp.zeros((head_count, group_pos.shape[0]), jnp.float32),
            )
            for group_queries, group_pos, group_begin in groups
        )
    )
    offset_row = jnp.int32(0)
    keys_piece = lax.all_gather(attn_key, "ctx", axis=0, tiled=True)
    values_piece = lax.all_gather(hyena_mix, "ctx", axis=0, tiled=True)
    key_rows = keys_piece.shape[0]
    key_heads = keys_piece.reshape(key_rows, head_count, HEAD_DIM)
    value_heads = values_piece.reshape(key_rows, head_count, HEAD_DIM)
    key_pos = jnp.arange(key_rows, dtype=jnp.int32)
    updated = []
    for state_now, (group_queries, group_pos, group_begin) in zip(initial, groups):
        needed = (offset_row <= jnp.max(group_pos)) & (offset_row + key_rows > jnp.min(group_begin))
        update = partial(
            attend_update,
            queries=group_queries,
            query_pos=group_pos,
            query_begin=group_begin,
            key_heads=key_heads,
            value_heads=value_heads,
            key_pos=key_pos,
        )
        updated.append(lax.cond(needed, update, keep_state, state_now))
    results = tuple(updated)
    outputs = []
    for weighted, running_max, weight_sum in results:
        finished = (weighted / weight_sum[:, :, None]).astype(jnp.bfloat16)
        outputs.append(finished.transpose(1, 0, 2).reshape(weighted.shape[1], channels))
    attended = outputs[0]
    return (hyena_mix, attended)


def solution(mesh):
    return jax.shard_map(
        per_device,
        mesh=mesh,
        in_specs=(
            P(("rep", "ctx"), ("ch", "sub")),
            P(("rep", "ctx"), ("ch", "sub")),
            P(("rep", "ctx"), ("ch", "sub")),
            P(("ch", "sub"), None),
            P(("ch", "sub")),
            P(("rep", "ctx"), ("ch", "sub")),
            P(("rep", "ctx"), ("ch", "sub")),
            P("rep"),
        ),
        out_specs=(P(("rep", "ctx"), ("ch", "sub")), P(("rep", "ctx"), ("ch", "sub"))),
        check_vma=False,
    )
```

profile of v0, /device:TPU:0, one launch (start us, length us, event | category | flops | bytes accessed | tf_op | source)
XLA Modules:
  0.0 359.8 jit_solution(4277070580375410780)
XLA Ops:
  7.2 0.0 all-gather.3.cloned.1.call-start
  7.2 0.7 all-gather.3.cloned.1.call-update
  7.9 0.0 all-gather.5.cloned.1.call-start
  8.0 2.5 multiply_convert_fusion
  10.5 1.0 slice.12
  11.5 5.7 %collective-permute-start = (bf16[127,2048]{1,0:T(8,128)(2,1)}, bf16[127,2048]{1,0:T(8,128)(2,1)}, u32[]{:S(2)}, u32[]{:S(2)}) collective-permute-start(bf16[127,2048]{1,0:T(8,128)(2,1)} %slice.12), channel_id=1, source_target_pairs={{0,4},{4,8},{8,12},{1,5},{5,9},{9,13},{2,6},{6,10},{10,14},{3,7},{... | collective-permute-start | bytes 1560584 | tf_op jit(solution)/shard_map/ppermute | solution.py:14
  17.2 0.1 convert_reduce_fusion
  17.3 0.1 broadcast_in_dim.88
  17.4 1.5 rev.3
  18.9 0.9 copy.43
  19.8 0.7 fusion.24
  20.5 0.5 fusion.26
  21.1 13.9 %collective-permute-done = bf16[127,2048]{1,0:T(8,128)(2,1)} collective-permute-done((bf16[127,2048]{1,0:T(8,128)(2,1)}, bf16[127,2048]{1,0:T(8,128)(2,1)}, u32[]{:S(2)}, u32[]{:S(2)}) %collective-permute-start) | collective-permute-done | bytes 520224 | tf_op jit(solution)/shard_map/ppermute | solution.py:14
  34.9 1.9 copy_dynamic-update-slice_fusion.1
  36.8 2.6 copy_dynamic-update-slice_fusion
  39.4 8.6 %broadcast_select_fusion.1 = (bf16[1,511,2048]{2,0,1:T(2,128)(2,1)S(1)}, bf16[1,511,2048]{2,0,1:T(2,128)(2,1)S(1)}) fusion(bf16[1,511,2048]{2,0,1:T(2,128)(2,1)S(1)} %copy_dynamic-update-slice_fusion, pred[511]{0:T(512)(128)(4,1)S(1)} %get-tuple-element.33, pred[511]{0:T(512)(128)(4,1)S(1)} %broadcast_compare_fusion), kind=kLoop, calls=%fused_computation.18 | loop fusion | flops 2093056 | bytes 6280190 | tf_op jit(solution)/shard_map/jit(_where)/select_n | solution.py:32
  48.1 9.6 %fusion.39 = bf16[2,511,2048]{2,0,1:T(2,128)(2,1)S(1)} fusion(bf16[1,511,2048]{2,0,1:T(2,128)(2,1)S(1)} %get-tuple-element.40, bf16[1,511,2048]{2,0,1:T(2,128)(2,1)S(1)} %get-tuple-element.39), kind=kLoop, calls=%fused_computation.20.clone.1 | loop fusion | flops 8372224 | bytes 8372224 | tf_op jit(solution)/shard_map/conv_general_dilated | solution.py:35
  57.7 90.8 %fusion.14 = f32[2,384,2048]{2,0,1:T(2,128)} fusion(bf16[128,1,2048]{2,1,0:T(2,128)(2,1)S(1)} %copy.43, bf16[2,511,2048]{2,0,1:T(2,128)(2,1)S(1)} %fusion.39), kind=kOutput, calls=%fused_computation.19 | convolution fusion | flops 402653184 | bytes 11001856 | tf_op jit(solution)/shard_map/conv_general_dilated | solution.py:35
  148.5 13.9 %fusion.30 = (f32[1,384,2048]{2,0,1:T(1,128)}, f32[1,384,2048]{2,0,1:T(1,128)}) fusion(f32[2,384,2048]{2,0,1:T(2,128)} %fusion.14), kind=kLoop, calls=%fused_computation.54 | loop fusion | bytes 12582912 | tf_op jit(solution)/shard_map/slice | solution.py:86
  162.5 6.9 %fusion.21 = bf16[384,2048]{1,0:T(8,128)(2,1)} fusion(f32[1,384,2048]{2,0,1:T(1,128)} %get-tuple-element.38, f32[1,384,2048]{2,0,1:T(1,128)} %get-tuple-element.37, bf16[384,2048]{1,0:T(8,128)(2,1)S(1)} %copy-done.1, bf16[384,2048]{1,0:T(8,128)(2,1)S(1)} %copy-done.4, f32[2048]{0:T(1024)S(1)} %copy-done.9, pred[384]{0:T(512)(128)(4,1)S(1)} %copy-done.10), kind=kLoop, calls=%fused_computation.27 | loop fusion | flops 5505024 | bytes 11018624 | tf_op jit(solution)/shard_map/convert_element_type | solution.py:90
  169.4 0.0 all-gather.5.cloned.1.call-update
  169.4 0.6 fusion.28
  170.7 0.6 reduce_min.9
  172.0 0.0 all-gather.3.cloned.1.call-done
  172.0 121.9 %all-gather.5.cloned.1.call-done = bf16[1536,2048]{1,0:T(8,128)(2,1)} async-done(((bf16[384,2048]{1,0:T(8,128)(2,1)}), bf16[1536,2048]{1,0:T(8,128)(2,1)}) %all-gather.5.cloned.1.call-update) | async-done | bytes 6291472 | tf_op jit(solution)/shard_map/all_gather | solution.py:110
  293.9 57.2 %conditional.1 = (f32[16,384,128]{2,1,0:T(8,128)S(1)}, f32[16,384]{1,0:T(8,128)S(1)}) conditional(s32[]{:T(128)} %convert_element_type.41, () %tuple.16, (s32[1536]{0:T(1024)S(1)}, s32[1536]{0:T(1024)S(1)}, s32[384]{0:T(512)S(1)}, s32[384]{0:T(512)S(1)}, bf16[384,2048]{1,0:T(8,128)(2,1)}, /*index=5*/bf16[1536,2048]{1,0:T(8,128)(2,1)}, ...), branch_computations={%region_5.6_spmd, %region_6.9_spmd} | conditional | flops 4937410560 | bytes 137788496 | solution.py:127
  293.9 0.5 compare_and_fusion
  294.5 0.0 copy-start.2
  294.5 18.5 %select_reduce_fusion = (f32[16,384]{1,0:T(8,128)S(1)}, f32[16,384,1536]{2,1,0:T(8,128)}) fusion(pred[384,1536]{1,0:T(8,128)(4,1)S(1)} %compare_and_fusion, bf16[1536,2048]{1,0:T(8,128)(2,1)} %get-tuple-element.21, bf16[384,2048]{1,0:T(8,128)(2,1)} %get-tuple-element.30), kind=kOutput, calls=%fused_computation.1 | convolution fusion | flops 2444224512 | bytes 46227456 | tf_op jit(solution)/shard_map/cond/branch_1_fun/qhd,khd->hqk/dot_general | solution.py:50
  313.0 21.0 %fusion.2 = f32[16,384,128]{2,1,0:T(8,128)S(1)} fusion(f32[16,384,1536]{2,1,0:T(8,128)} %get-tuple-element.36, f32[16,384]{1,0:T(8,128)S(1)} %broadcast_maximum_fusion, pred[384,1536]{1,0:T(8,128)(4,1)} %copy-done.2, bf16[1536,2048]{1,0:T(8,128)(2,1)} %get-tuple-element.22), kind=kOutput, calls=%fused_computation.4 | convolution fusion | flops 2453667840 | bytes 47800320 | tf_op jit(solution)/shard_map/cond/branch_1_fun/hqk,khd->hqd/dot_general | solution.py:56
  334.0 17.1 %fusion = f32[16,384]{1,0:T(8,128)S(1)} fusion(f32[16,384,1536]{2,1,0:T(8,128)} %get-tuple-element.36, f32[16,384]{1,0:T(8,128)S(1)} %broadcast_maximum_fusion, pred[384,1536]{1,0:T(8,128)(4,1)S(1)} %copy-done.3), kind=kLoop, calls=%fused_computation.2 | loop fusion | flops 37742592 | bytes 38387712 | tf_op jit(solution)/shard_map/cond/branch_1_fun/reduce_sum | solution.py:62
  351.1 1.9 copy_bitcast_fusion.1
  (29 shorter events, 0.1 us)
Async XLA Ops:
  7.2 10.1 %copy-start.11 = (s32[4]{0:T(128)S(1)}, s32[4]{0:T(128)}, u32[]{:S(2)}) copy-start(s32[4]{0:T(128)} %param.17) | copy-start | bytes 52
  7.2 10.2 %copy-start.5 = (bf16[128,128]{1,0:T(8,128)(2,1)S(1)}, bf16[128,128]{1,0:T(8,128)(2,1)}, u32[]{:S(2)}) copy-start(bf16[128,128]{1,0:T(8,128)(2,1)} %param.13) | copy-start | bytes 98308
  7.2 164.8 %all-gather.3.cloned.1.call-start = ((), (), s32[]{:S(2)}) async-start(), calls=%async_computation | async-start | bytes 7864320 | tf_op jit(solution)/shard_map/all_gather | solution.py:109
  7.9 286.0 %all-gather.5.cloned.1.call-start = ((), (), s32[]{:S(2)}) async-start(), calls=%async_computation.1 | async-start | bytes 7864320 | tf_op jit(solution)/shard_map/all_gather | solution.py:110
  10.5 28.9 %copy-start = (bf16[384,2048]{1,0:T(8,128)(2,1)}, bf16[384,2048]{1,0:T(8,128)(2,1)S(1)}, u32[]{:S(2)}) copy-start(bf16[384,2048]{1,0:T(8,128)(2,1)S(1)} %multiply_convert_fusion) | copy-start | bytes 4718596
  11.5 23.4 %collective-permute-start = (bf16[127,2048]{1,0:T(8,128)(2,1)}, bf16[127,2048]{1,0:T(8,128)(2,1)}, u32[]{:S(2)}, u32[]{:S(2)}) collective-permute-start(bf16[127,2048]{1,0:T(8,128)(2,1)} %slice.12), channel_id=1, source_target_pairs={{0,4},{4,8},{8,12},{1,5},{5,9},{9,13},{2,6},{6,10},{10,14},{3,7},{... | collective-permute-start | bytes 1560584 | tf_op jit(solution)/shard_map/ppermute | solution.py:14
  17.2 22.2 %copy-start.6 = (s32[384]{0:T(512)}, s32[384]{0:T(512)S(1)}, u32[]{:S(2)}) copy-start(s32[384]{0:T(512)S(1)} %iota_add_fusion.1) | copy-start | bytes 4612
  148.5 13.9 %copy-start.1 = (bf16[384,2048]{1,0:T(8,128)(2,1)S(1)}, bf16[384,2048]{1,0:T(8,128)(2,1)}, u32[]{:S(2)}) copy-start(bf16[384,2048]{1,0:T(8,128)(2,1)} %copy-done) | copy-start | bytes 4718596
  148.5 13.9 %copy-start.4 = (bf16[384,2048]{1,0:T(8,128)(2,1)S(1)}, bf16[384,2048]{1,0:T(8,128)(2,1)}, u32[]{:S(2)}) copy-start(bf16[384,2048]{1,0:T(8,128)(2,1)} %param.10) | copy-start | bytes 4718596
  148.5 13.9 %copy-start.9 = (f32[2048]{0:T(1024)S(1)}, f32[2048]{0:T(1024)}, u32[]{:S(2)}) copy-start(f32[2048]{0:T(1024)} %param.14) | copy-start | bytes 24580
  148.5 13.9 %copy-start.10 = (pred[384]{0:T(512)(128)(4,1)S(1)}, pred[384]{0:T(512)(128)(4,1)}, u32[]{:S(2)}) copy-start(pred[384]{0:T(512)(128)(4,1)} %fusion.26) | copy-start | bytes 1156
  162.5 8.2 %copy-start.8 = (s32[384]{0:T(512)S(1)}, s32[384]{0:T(512)}, u32[]{:S(2)}) copy-start(s32[384]{0:T(512)} %get-tuple-element.31) | copy-start | bytes 4612
  162.5 131.5 %copy-start.7 = (s32[384]{0:T(512)S(1)}, s32[384]{0:T(512)}, u32[]{:S(2)}) copy-start(s32[384]{0:T(512)} %copy-done.6) | copy-start | bytes 4612
  294.5 18.5 %copy-start.2 = (pred[384,1536]{1,0:T(8,128)(4,1)}, pred[384,1536]{1,0:T(8,128)(4,1)S(1)}, u32[]{:S(2)}) copy-start(pred[384,1536]{1,0:T(8,128)(4,1)S(1)} %compare_and_fusion) | copy-start | bytes 1769476 | tf_op jit(solution)/shard_map/cond
  313.0 21.0 %copy-start.3 = (pred[384,1536]{1,0:T(8,128)(4,1)S(1)}, pred[384,1536]{1,0:T(8,128)(4,1)}, u32[]{:S(2)}) copy-start(pred[384,1536]{1,0:T(8,128)(4,1)} %copy-done.2) | copy-start | bytes 1769476 | tf_op jit(solution)/shard_map/cond
Sparse Core Ops, SparseCore 0:
  9.6 119.8 all-gather.2
  169.5 124.3 all-gather.4
where the time goes:
time: 360 us
  waiting for transfers between devices  136 us (38%)
  matrix products  130 us (36%)
  other arithmetic  49.8 us (14%)
  local copies, waits for them, and re-layouts  21.9 us (6%)
  between operations  15.5 us (4%)
  starting transfers between devices  5.79 us (2%)
    all_gather x1, waiting for transfers between devices, per_device(): values_piece = lax.all_gather(hyena_mix, 'ctx', axis=0, tiled=True)  122 us
    conv_general_dilated x1, matrix products, grouped_filter(): lax.conv_general_dilated(stacked, kernel, (1,), [(left_pad, 0)], dimensio...  90.8 us
    dot_general x1, matrix products, attend_update(): jnp.einsum('hqk,khd->hqd', weights.astype(jnp.bfloat16), value_heads, pre...  21 us
    dot_general x1, matrix products, attend_update(): jnp.einsum('qhd,khd->hqk', queries, key_heads, preferred_element_type=jnp...  18.5 us
    reduce_sum x1, other arithmetic, attend_update(): return (mixed, new_max, jnp.sum(weights, axis=2))  17.1 us
    slice x1, local copies, waits for them, and re-layouts, per_device(): both_parities[1]  13.9 us
    ppermute x1, waiting for transfers between devices, passed_along(): return lax.ppermute(value, axis, pairs)  13.9 us
    conv_general_dilated x1, other arithmetic, grouped_filter(): lax.conv_general_dilated(stacked, kernel, (1,), [(left_pad, 0)], dimensio...  9.64 us
  transfers between devices with their start and end apart: 3, of which 2 were waited for; matrix products, arithmetic and copies ran while one was open for 40% of the time, Pallas kernels for 0%

commit v1 on v0

--- a/solution.py
+++ b/solution.py
@@ -4,6 +4,7 @@
 import jax.numpy as jnp
 from jax import lax
 from jax.sharding import PartitionSpec as P
+from jax.lax import all_gather
 
 HEAD_DIM = 128
 
@@ -106,8 +107,11 @@
         )
     )
     offset_row = jnp.int32(0)
-    keys_piece = lax.all_gather(attn_key, "ctx", axis=0, tiled=True)
-    values_piece = lax.all_gather(hyena_mix, "ctx", axis=0, tiled=True)
+    keys_piece, values_piece = jnp.split(
+        all_gather(jnp.concatenate([attn_key, hyena_mix], 1), axis_name="ctx", axis=0, tiled=True),
+        [attn_key.shape[1]],
+        1,
+    )
     key_rows = keys_piece.shape[0]
     key_heads = keys_piece.reshape(key_rows, head_count, HEAD_DIM)
     value_heads = values_piece.reshape(key_rows, head_count, HEAD_DIM)

time: 360 us -> 473 us (1.31)
  waiting for transfers between devices: 136 us -> 225 us
  local copies, waits for them, and re-layouts: 21.9 us -> 50 us
    all_gather x2 -> x1, waiting for transfers between devices: 122 us -> 219 us  [per_device(): all_gather(jnp.concatenate([attn_key, hyena_mix], 1), axis_name='ctx', ax...]
    another operation x0 -> x1, local copies, waits for them, and re-layouts: none -> 16.7 us
    split x0 -> x1, local copies, waits for them, and re-layouts: none -> 10.3 us  [per_device(): jnp.split(all_gather(jnp.concatenate([attn_key, hyena_mix], 1), axis_name...]
    ppermute x1, waiting for transfers between devices: 13.9 us -> 6.22 us  [passed_along(): return lax.ppermute(value, axis, pairs)]
  transfers between devices with their start and end apart: 3 -> 2, of which waited for: 2 -> 2; matrix products, arithmetic and copies ran while one was open for 40% -> 1% of each run, Pallas kernels for 0% -> 0%
where the time goes in v1:
time: 473 us
  waiting for transfers between devices  225 us (48%)
  matrix products  126 us (27%)
  other arithmetic  50.8 us (11%)
  local copies, waits for them, and re-layouts  50 us (11%)
  between operations  15.4 us (3%)
  starting transfers between devices  5.76 us (1%)
    all_gather x1, waiting for transfers between devices, per_device(): all_gather(jnp.concatenate([attn_key, hyena_mix], 1), axis_name='ctx', ax...  219 us
    conv_general_dilated x1, matrix products, grouped_filter(): lax.conv_general_dilated(stacked, kernel, (1,), [(left_pad, 0)], dimensio...  90.8 us
    dot_general x1, matrix products, attend_update(): jnp.einsum('qhd,khd->hqk', queries, key_heads, preferred_element_type=jnp...  18 us
    reduce_sum x1, other arithmetic, attend_update(): return (mixed, new_max, jnp.sum(weights, axis=2))  17.2 us
    dot_general x1, matrix products, attend_update(): jnp.einsum('hqk,khd->hqd', weights.astype(jnp.bfloat16), value_heads, pre...  17.1 us
    another operation x1, local copies, waits for them, and re-layouts  16.7 us
    slice x1, local copies, waits for them, and re-layouts, per_device(): both_parities[1]  13.9 us
    split x1, local copies, waits for them, and re-layouts, per_device(): jnp.split(all_gather(jnp.concatenate([attn_key, hyena_mix], 1), axis_name...  10.3 us
  transfers between devices with their start and end apart: 2, of which 2 were waited for; matrix products, arithmetic and copies ran while one was open for 1% of the time, Pallas kernels for 0%

profile of v1, /device:TPU:0, one launch (start us, length us, event | category | flops | bytes accessed | tf_op | source)
XLA Modules:
  0.0 472.8 jit_solution(14397683990399156630)
XLA Ops:
  7.2 0.0 all-gather.2.cloned.1.call-start
  7.2 2.5 multiply_convert_fusion
  9.7 1.0 slice.12
  10.8 5.7 %collective-permute-start = (bf16[127,2048]{1,0:T(8,128)(2,1)}, bf16[127,2048]{1,0:T(8,128)(2,1)}, u32[]{:S(2)}, u32[]{:S(2)}) collective-permute-start(bf16[127,2048]{1,0:T(8,128)(2,1)} %slice.12), channel_id=1, source_target_pairs={{0,4},{4,8},{8,12},{1,5},{5,9},{9,13},{2,6},{6,10},{10,14},{3,7},{... | collective-permute-start | bytes 1560584 | tf_op jit(solution)/shard_map/ppermute | solution.py:15
  16.5 0.6 iota_add_fusion.1
  17.1 0.1 convert_reduce_fusion
  17.2 0.1 broadcast_in_dim.88
  17.3 1.5 rev.3
  18.8 0.9 copy.43
  19.7 0.7 fusion.20
  20.4 0.5 fusion.22
  20.9 6.2 %collective-permute-done = bf16[127,2048]{1,0:T(8,128)(2,1)} collective-permute-done((bf16[127,2048]{1,0:T(8,128)(2,1)}, bf16[127,2048]{1,0:T(8,128)(2,1)}, u32[]{:S(2)}, u32[]{:S(2)}) %collective-permute-start) | collective-permute-done | bytes 520224 | tf_op jit(solution)/shard_map/ppermute | solution.py:15
  27.2 1.8 copy_dynamic-update-slice_fusion.1
  29.0 2.6 copy_dynamic-update-slice_fusion
  31.6 8.6 %broadcast_select_fusion.1 = (bf16[1,511,2048]{2,0,1:T(2,128)(2,1)S(1)}, bf16[1,511,2048]{2,0,1:T(2,128)(2,1)S(1)}) fusion(bf16[1,511,2048]{2,0,1:T(2,128)(2,1)S(1)} %copy_dynamic-update-slice_fusion, pred[511]{0:T(512)(128)(4,1)S(1)} %get-tuple-element.51, pred[511]{0:T(512)(128)(4,1)S(1)} %broadcast_compare_fusion), kind=kLoop, calls=%fused_computation.14 | loop fusion | flops 2093056 | bytes 6280190 | tf_op jit(solution)/shard_map/jit(_where)/select_n | solution.py:33
  40.3 9.6 %fusion.36 = bf16[2,511,2048]{2,0,1:T(2,128)(2,1)S(1)} fusion(bf16[1,511,2048]{2,0,1:T(2,128)(2,1)S(1)} %get-tuple-element.60, bf16[1,511,2048]{2,0,1:T(2,128)(2,1)S(1)} %get-tuple-element.59), kind=kLoop, calls=%fused_computation.16.clone.1 | loop fusion | flops 8372224 | bytes 8372224 | tf_op jit(solution)/shard_map/conv_general_dilated | solution.py:36
  49.9 90.8 %fusion.10 = f32[2,384,2048]{2,0,1:T(2,128)} fusion(bf16[128,1,2048]{2,1,0:T(2,128)(2,1)S(1)} %copy.43, bf16[2,511,2048]{2,0,1:T(2,128)(2,1)S(1)} %fusion.36), kind=kOutput, calls=%fused_computation.15 | convolution fusion | flops 402653184 | bytes 11001856 | tf_op jit(solution)/shard_map/conv_general_dilated | solution.py:36
  140.8 13.9 %fusion.27 = (f32[1,384,2048]{2,0,1:T(1,128)}, f32[1,384,2048]{2,0,1:T(1,128)}) fusion(f32[2,384,2048]{2,0,1:T(2,128)} %fusion.10), kind=kLoop, calls=%fused_computation.52 | loop fusion | bytes 12582912 | tf_op jit(solution)/shard_map/slice | solution.py:87
  154.7 5.9 %fusion.17 = bf16[384,2048]{1,0:T(8,128)(2,1)S(1)} fusion(f32[1,384,2048]{2,0,1:T(1,128)} %get-tuple-element.58, f32[1,384,2048]{2,0,1:T(1,128)} %get-tuple-element.57, bf16[384,2048]{1,0:T(8,128)(2,1)S(1)} %copy-done.1, bf16[384,2048]{1,0:T(8,128)(2,1)S(1)} %copy-done.5, f32[2048]{0:T(1024)S(1)} %copy-done.11, pred[384]{0:T(512)(128)(4,1)S(1)} %copy-done.12), kind=kLoop, calls=%fused_computation.24 | loop fusion | flops 5505024 | bytes 11018624 | tf_op jit(solution)/shard_map/convert_element_type | solution.py:91
  160.6 1.1 copy-done.3
  161.7 2.0 pad_maximum_fusion
  163.7 0.0 all-gather.2.cloned.1.call-update
  164.3 0.6 reduce_min.9
  165.6 218.7 %all-gather.2.cloned.1.call-done = bf16[1536,4096]{1,0:T(8,128)(2,1)} async-done(((bf16[384,4096]{1,0:T(8,128)(2,1)}), bf16[1536,4096]{1,0:T(8,128)(2,1)}) %all-gather.2.cloned.1.call-update) | async-done | bytes 12582928 | tf_op jit(solution)/shard_map/all_gather | solution.py:111
  384.3 79.8 %conditional.1 = (f32[16,384,128]{2,1,0:T(8,128)S(1)}, f32[16,384]{1,0:T(8,128)S(1)}) conditional(s32[]{:T(128)} %convert_element_type.41, () %tuple.16, (s32[1536]{0:T(1024)S(1)}, s32[1536]{0:T(1024)S(1)}, s32[384]{0:T(512)S(1)}, s32[384]{0:T(512)S(1)}, bf16[384,2048]{1,0:T(8,128)(2,1)}, /*index=5*/bf16[1536,4096]{1,0:T(8,128)(2,1)}) %tuple.34), branch_computations={%region_5.6_spmd, %region_6.9_spmd} | conditional | flops 4937410560 | bytes 192052304 | solution.py:131
  384.3 16.7 %copy.45 = bf16[1536,4096]{0,1:T(8,128)(2,1)} copy(bf16[1536,4096]{1,0:T(8,128)(2,1)} %get-tuple-element.48) | data formatting | bytes 25165824 | tf_op jit(solution)/shard_map
  400.9 10.3 %fusion.26 = (bf16[1536,2048]{0,1:T(8,128)(2,1)}, bf16[1536,2048]{0,1:T(8,128)(2,1)}) fusion(bf16[1536,4096]{0,1:T(8,128)(2,1)} %copy.45), kind=kLoop, calls=%fused_computation.51 | loop fusion | bytes 25165824 | tf_op jit(solution)/shard_map/split | solution.py:110
  411.2 0.5 compare_and_fusion
  411.8 18.0 %select_reduce_fusion = (f32[16,384]{1,0:T(8,128)S(1)}, f32[16,384,1536]{2,1,0:T(8,128)}) fusion(pred[384,1536]{1,0:T(8,128)(4,1)S(1)} %compare_and_fusion, bf16[1536,16,128]{0,2,1:T(8,128)(2,1)} %bitcast.40, bf16[384,2048]{1,0:T(8,128)(2,1)S(1)} %copy-done.4), kind=kOutput, calls=%fused_computation.1 | convolution fusion | flops 2444224512 | bytes 46227456 | tf_op jit(solution)/shard_map/cond/branch_1_fun/qhd,khd->hqk/dot_general | solution.py:51
  429.8 17.1 %fusion.2 = f32[16,384,128]{2,1,0:T(8,128)S(1)} fusion(bf16[1536,16,128]{0,2,1:T(8,128)(2,1)} %bitcast.42, f32[16,384,1536]{2,1,0:T(8,128)} %get-tuple-element.56, f32[16,384]{1,0:T(8,128)S(1)} %broadcast_maximum_fusion, pred[384,1536]{1,0:T(8,128)(4,1)} %copy-done.2), kind=kOutput, calls=%fused_computation.4 | convolution fusion | flops 2453667840 | bytes 47800320 | tf_op jit(solution)/shard_map/cond/branch_1_fun/hqk,khd->hqd/dot_general | solution.py:57
  446.9 17.2 %fusion = f32[16,384]{1,0:T(8,128)S(1)} fusion(f32[16,384,1536]{2,1,0:T(8,128)} %get-tuple-element.56, f32[16,384]{1,0:T(8,128)S(1)} %broadcast_maximum_fusion, pred[384,1536]{1,0:T(8,128)(4,1)} %copy-done.2), kind=kLoop, calls=%fused_computation.2 | loop fusion | flops 37742592 | bytes 38387712 | tf_op jit(solution)/shard_map/cond/branch_1_fun/reduce_sum | solution.py:63
  464.1 1.9 copy_bitcast_fusion.1
  (32 shorter events, 0.1 us)
Async XLA Ops:
  7.2 9.9 %copy-start.13 = (s32[4]{0:T(128)S(1)}, s32[4]{0:T(128)}, u32[]{:S(2)}) copy-start(s32[4]{0:T(128)} %param.17) | copy-start | bytes 52
  7.2 10.0 %copy-start.7 = (bf16[128,128]{1,0:T(8,128)(2,1)S(1)}, bf16[128,128]{1,0:T(8,128)(2,1)}, u32[]{:S(2)}) copy-start(bf16[128,128]{1,0:T(8,128)(2,1)} %param.13) | copy-start | bytes 98308
  7.2 377.1 %all-gather.2.cloned.1.call-start = ((), (), s32[]{:S(2)}) async-start(), calls=%async_computation | async-start | bytes 15728640 | tf_op jit(solution)/shard_map/all_gather | solution.py:111
  9.7 21.9 %copy-start = (bf16[384,2048]{1,0:T(8,128)(2,1)}, bf16[384,2048]{1,0:T(8,128)(2,1)S(1)}, u32[]{:S(2)}) copy-start(bf16[384,2048]{1,0:T(8,128)(2,1)S(1)} %multiply_convert_fusion) | copy-start | bytes 4718596
  10.8 16.4 %collective-permute-start = (bf16[127,2048]{1,0:T(8,128)(2,1)}, bf16[127,2048]{1,0:T(8,128)(2,1)}, u32[]{:S(2)}, u32[]{:S(2)}) collective-permute-start(bf16[127,2048]{1,0:T(8,128)(2,1)} %slice.12), channel_id=1, source_target_pairs={{0,4},{4,8},{8,12},{1,5},{5,9},{9,13},{2,6},{6,10},{10,14},{3,7},{... | collective-permute-start | bytes 1560584 | tf_op jit(solution)/shard_map/ppermute | solution.py:15
  17.1 14.5 %copy-start.8 = (s32[384]{0:T(512)}, s32[384]{0:T(512)S(1)}, u32[]{:S(2)}) copy-start(s32[384]{0:T(512)S(1)} %get-tuple-element.61) | copy-start | bytes 4612
  140.8 13.9 %copy-start.1 = (bf16[384,2048]{1,0:T(8,128)(2,1)S(1)}, bf16[384,2048]{1,0:T(8,128)(2,1)}, u32[]{:S(2)}) copy-start(bf16[384,2048]{1,0:T(8,128)(2,1)} %copy-done) | copy-start | bytes 4718596
  140.8 13.9 %copy-start.5 = (bf16[384,2048]{1,0:T(8,128)(2,1)S(1)}, bf16[384,2048]{1,0:T(8,128)(2,1)}, u32[]{:S(2)}) copy-start(bf16[384,2048]{1,0:T(8,128)(2,1)} %param.10) | copy-start | bytes 4718596
  140.8 13.9 %copy-start.11 = (f32[2048]{0:T(1024)S(1)}, f32[2048]{0:T(1024)}, u32[]{:S(2)}) copy-start(f32[2048]{0:T(1024)} %param.14) | copy-start | bytes 24580
  140.8 13.9 %copy-start.12 = (pred[384]{0:T(512)(128)(4,1)S(1)}, pred[384]{0:T(512)(128)(4,1)}, u32[]{:S(2)}) copy-start(pred[384]{0:T(512)(128)(4,1)} %fusion.22) | copy-start | bytes 1156
  154.7 7.0 %copy-start.6 = (bf16[384,2048]{1,0:T(8,128)(2,1)S(1)}, bf16[384,2048]{1,0:T(8,128)(2,1)}, u32[]{:S(2)}) copy-start(bf16[384,2048]{1,0:T(8,128)(2,1)} %param.16) | copy-start | bytes 4718596
  160.6 1.1 copy-start.3
  161.7 2.6 copy-start.10
  161.7 222.6 %copy-start.9 = (s32[384]{0:T(512)S(1)}, s32[384]{0:T(512)}, u32[]{:S(2)}) copy-start(s32[384]{0:T(512)} %copy-done.8) | copy-start | bytes 4612
  400.9 10.8 %copy-start.4 = (bf16[384,2048]{1,0:T(8,128)(2,1)S(1)}, bf16[384,2048]{1,0:T(8,128)(2,1)}, u32[]{:S(2)}) copy-start(bf16[384,2048]{1,0:T(8,128)(2,1)} %get-tuple-element.30) | copy-start | bytes 4718596 | tf_op jit(solution)/shard_map/cond
  411.8 18.0 %copy-start.2 = (pred[384,1536]{1,0:T(8,128)(4,1)}, pred[384,1536]{1,0:T(8,128)(4,1)S(1)}, u32[]{:S(2)}) copy-start(pred[384,1536]{1,0:T(8,128)(4,1)S(1)} %compare_and_fusion) | copy-start | bytes 1769476 | tf_op jit(solution)/shard_map/cond
Sparse Core Ops, SparseCore 0:
  163.9 220.3 all-gather.1
